TPU v7x, 32 devices: a whole 2x2x4 slice. The times are simulated.
32 devices in a mesh: row: 8 (over z, core), col: 4 (over y, x).
Axes of the slice: x: 2, y: 2, z: 4, core: 2. Of those that a mesh axis runs over, the one named last changes fastest.
Arguments:
- labels_prior: float32 [16, 65536], P(None, ('row', 'col')), may hold values from 0.05 to 1
- tiles: bfloat16 [7168, 128, 128], P(('row', 'col')), may hold values from 0 to 1
- tile_rows: int32 [7168], P(('row', 'col')), may hold values from 0 to 63, as said below
- tile_cols: int32 [7168], P(('row', 'col')), may hold values from 0 to 127, as said below
- tile_count: int32 [32], P(('row', 'col')), may hold values from 28 to 224, as said below
Outputs:
- scores: float32 [16, 65536], P(None, ('row', 'col'))
Inputs may be any that keep to these rules, and one draw needn't show every extreme that they name: `tile_rows`: block rows within a row group of 16 * 4 blocks; both ends occur. `tile_cols`: block columns within a column group of 16 * 8 blocks; both ends occur. `tile_count`: loads are skewed; some device uses all 224 slots.
All inputs are finite; a program needn't handle non-finite values.
Results may differ from a plain program's by a relative error of at most 0.0003.
Values may be sent and summed in bfloat16 or wider, within the bound.
A program may use at most 64 MiB of HBM per device.

v0:
```python
import jax
import jax.numpy as jnp
from jax import lax
from jax.sharding import PartitionSpec as P

ITERS = 2
spread_weight = 0.9


def local(labels_prior, tiles, tile_rows, tile_cols, tile_count):
    labels, piece = labels_prior.shape
    tile_size = tiles.shape[1]
    n_col = lax.axis_size("col")
    own_blocks = piece // tile_size
    group_blocks = n_col * own_blocks
    slot_total = tiles.shape[0]
    valid = (jnp.arange(slot_total, dtype=jnp.int32) < tile_count[0]).astype(jnp.float32)
    row_hot = (tile_rows[:, None] == jnp.arange(group_blocks, dtype=jnp.int32)[None, :]).astype(
        jnp.float32
    ) * valid[:, None]
    rowsum = jnp.sum(tiles, axis=2, dtype=jnp.float32)
    degree_part = jnp.einsum("sr,si->ri", row_hot, rowsum, precision=lax.Precision.HIGHEST).reshape(
        -1
    )
    current = labels_prior
    degree = lax.psum_scatter(degree_part, "col", scatter_dimension=0, tiled=True) + 1.0
    remaining = ITERS
    for step in range(remaining):
        rounded = current.astype(jnp.bfloat16)
        whole = lax.all_gather(rounded, "row", axis=1, tiled=True)
        blocks = whole.reshape(labels, -1, tile_size)
        picked = jnp.take(blocks, tile_cols, axis=1)
        terms = jnp.einsum("lsj,sij->sli", picked, tiles, preferred_element_type=jnp.float32)
        sums = lax.psum_scatter(
            jnp.einsum("sr,sli->lri", row_hot, terms, precision=lax.Precision.HIGHEST).reshape(
                labels, -1
            ),
            "col",
            scatter_dimension=1,
            tiled=True,
        )
        current = (
            spread_weight * (sums + current) / degree[None, :]
            + (1.0 - spread_weight) * labels_prior
        )
    return current


def solution(mesh):
    in_specs = (
        P(None, ("row", "col")),
        P(("row", "col"), None, None),
        P(("row", "col")),
        P(("row", "col")),
        P(("row", "col")),
    )
    out_specs = P(None, ("row", "col"))
    return jax.shard_map(local, mesh=mesh, in_specs=in_specs, out_specs=out_specs, check_vma=False)
```

profile of v0, /device:TPU:0, one launch (start us, length us, event | category | flops | bytes accessed | tf_op | source)
XLA Modules:
  0.0 121.5 jit_solution(1303454846587029499)
XLA Ops:
  6.5 0.0 reduce-scatter.3.cloned.1.call-start
  6.5 0.7 compare_and_fusion
  7.2 0.7 compare_select_fusion
  8.6 0.9 convert_element_type.17
  9.5 16.6 %all_gather.6 = bf16[16,16384]{1,0:T(8,128)(2,1)S(1)} all-gather(bf16[16,2048]{1,0:T(8,128)(2,1)S(1)} %convert_element_type.17), channel_id=1, replica_groups=mesh['row'=8,'col'=4] {'row'}, dimensions={1}, use_global_device_ids=true | all-gather | bytes 589824 | tf_op jit(solution)/shard_map/all_gather | solution.py:30
  26.1 0.1 copy_bitcast_fusion.3
  26.2 0.8 gather_fusion
  27.0 0.0 copy-start.2
  27.0 6.2 %fusion.6 = f32[224,16,128]{2,1,0:T(8,128)S(1)} fusion(bf16[224,128,128]{2,1,0:T(8,128)(2,1)} %param.8, bf16[224,16,128]{2,1,0:T(8,128)(2,1)S(1)} %gather_fusion, pred[224]{0:T(512)(128)(4,1)S(1)} %compare_and_fusion), kind=kOutput, calls=%fused_computation.10 | convolution fusion | flops 117899264 | bytes 10092768 | tf_op jit(solution)/shard_map/lsj,sij->sli/dot_general | solution.py:33
  33.2 0.0 copy-done.2
  33.2 0.0 copy-start.3
  33.2 1.8 %fusion.2 = f32[16,128,64]{1,2,0:T(8,128)S(1)} fusion(f32[224,16,128]{2,1,0:T(8,128)S(1)} %fusion.6, f32[224]{0:T(256)S(1)} %compare_convert_fusion, s32[224]{0:T(256)S(1)} %copy-done.2), kind=kOutput, calls=%fused_computation.5 | convolution fusion | flops 352350208 | bytes 2361088 | tf_op jit(solution)/shard_map/sr,sli->lri/dot_general | solution.py:35
  35.0 1.1 copy.27
  36.1 0.0 reduce-scatter.3.cloned.1.call-update
  36.1 0.0 reduce-scatter.5.cloned.1.call-start
  36.2 0.0 copy-done.3
  36.2 0.6 dynamic-slice
  37.4 0.0 copy-start
  37.4 5.1 %convert_reduce_fusion = f32[224,128]{1,0:T(8,128)S(1)} fusion(bf16[224,128,128]{2,1,0:T(8,128)(2,1)} %param.8), kind=kLoop, calls=%fused_computation.2 | loop fusion | flops 7311360 | bytes 7454720 | tf_op jit(solution)/shard_map/reduce_sum | solution.py:21
  42.5 0.3 convolution_bitcast_fusion
  42.8 16.6 %all-reduce = f32[8192]{0:T(1024)S(1)} all-reduce(f32[8192]{0:T(1024)S(1)} %convolution_bitcast_fusion), channel_id=3, replica_groups=mesh['row'=8,'col'=4] {'col'}, use_global_device_ids=true, to_apply=%region_2.0.clone | all-reduce | flops 8192 | bytes 65536
  59.4 2.7 %reduce-scatter.3.cloned.1.call-done = f32[16,2048]{1,0:T(8,128)} async-done(((f32[16,8192]{1,0:T(8,128)}), f32[16,2048]{1,0:T(8,128)}) %reduce-scatter.3.cloned.1.call-update) | async-done | bytes 131088 | tf_op jit(solution)/shard_map/reduce_scatter | solution.py:34
  62.1 0.0 copy-done
  62.1 0.9 fusion.24
  63.1 14.8 %all_gather.7 = bf16[16,16384]{1,0:T(8,128)(2,1)S(1)} all-gather(bf16[16,2048]{1,0:T(8,128)(2,1)S(1)} %fusion.24), channel_id=1, replica_groups=mesh['row'=8,'col'=4] {'row'}, dimensions={1}, use_global_device_ids=true | all-gather | bytes 589824 | tf_op jit(solution)/shard_map/all_gather | solution.py:30
  77.8 0.1 copy_bitcast_fusion.2
  77.9 0.8 gather_fusion.1
  78.8 6.2 %fusion.4 = f32[224,16,128]{2,1,0:T(8,128)S(1)} fusion(bf16[224,128,128]{2,1,0:T(8,128)(2,1)} %param.8, bf16[224,16,128]{2,1,0:T(8,128)(2,1)S(1)} %gather_fusion.1, pred[224]{0:T(512)(128)(4,1)S(1)} %compare_and_fusion), kind=kOutput, calls=%fused_computation.8 | convolution fusion | flops 117899264 | bytes 10092768 | tf_op jit(solution)/shard_map/lsj,sij->sli/dot_general | solution.py:33
  84.9 0.0 copy-start.1
  84.9 1.8 %fusion = f32[16,128,64]{1,2,0:T(8,128)S(1)} fusion(f32[224,16,128]{2,1,0:T(8,128)S(1)} %fusion.4, f32[224]{0:T(256)S(1)} %compare_convert_fusion, s32[224]{0:T(256)S(1)} %copy-done.2), kind=kOutput, calls=%fused_computation.3 | convolution fusion | flops 352350208 | bytes 2361088 | tf_op jit(solution)/shard_map/sr,sli->lri/dot_general | solution.py:35
  86.7 1.1 copy.26
  87.8 0.0 reduce-scatter.5.cloned.1.call-update
  87.9 25.1 %reduce-scatter.5.cloned.1.call-done = f32[16,2048]{1,0:T(8,128)} async-done(((f32[16,8192]{1,0:T(8,128)}), f32[16,2048]{1,0:T(8,128)}) %reduce-scatter.5.cloned.1.call-update) | async-done | bytes 131088 | tf_op jit(solution)/shard_map/reduce_scatter | solution.py:34
  113.0 0.0 copy-done.1
  113.0 1.6 %divide_add_fusion = f32[16,2048]{1,0:T(8,128)} fusion(f32[16,2048]{1,0:T(8,128)} %reduce-scatter.5.cloned.1.call-done, f32[16,2048]{1,0:T(8,128)S(1)} %copy-done, f32[2048]{0:T(1024)S(1)} %dynamic-slice_add_fusion, f32[16,2048]{1,0:T(8,128)S(1)} %copy-done.1), kind=kLoop, calls=%fused_computation.22 | loop fusion | flops 294912 | bytes 532480 | tf_op jit(solution)/shard_map/add | solution.py:43
  (3 shorter events, 0.0 us)
Async XLA Ops:
  6.5 55.6 %reduce-scatter.3.cloned.1.call-start = ((), (), s32[]{:S(2)}) async-start(), calls=%async_computation.2 | async-start | bytes 655360 | tf_op jit(solution)/shard_map/reduce_scatter | solution.py:34
  27.0 6.2 %copy-start.2 = (s32[224]{0:T(256)S(1)}, s32[224]{0:T(256)}, u32[]{:S(2)}) copy-start(s32[224]{0:T(256)} %param.9) | copy-start | bytes 2692
  33.2 3.0 %copy-start.3 = (u32[32]{0:T(128)S(1)}, u32[32]{0:T(128)}, u32[]{:S(2)}) copy-start(u32[32]{0:T(128)} %constant.22) | copy-start | bytes 388
  36.1 76.9 %reduce-scatter.5.cloned.1.call-start = ((), (), s32[]{:S(2)}) async-start(), calls=%async_computation.3 | async-start | bytes 655360 | tf_op jit(solution)/shard_map/reduce_scatter | solution.py:34
  37.4 24.7 %copy-start = (f32[16,2048]{1,0:T(8,128)S(1)}, f32[16,2048]{1,0:T(8,128)}, u32[]{:S(2)}) copy-start(f32[16,2048]{1,0:T(8,128)} %param.7) | copy-start | bytes 393220
  84.9 28.1 %copy-start.1 = (f32[16,2048]{1,0:T(8,128)S(1)}, f32[16,2048]{1,0:T(8,128)}, u32[]{:S(2)}) copy-start(f32[16,2048]{1,0:T(8,128)} %reduce-scatter.3.cloned.1.call-done) | copy-start | bytes 393220
Sparse Core Ops, SparseCore 0:
  36.2 25.8 reduce-scatter.2
  88.0 24.9 reduce-scatter.4
where the time goes:
time: 122 us; the launch traced here: 121 us
  blocking collectives  48 us (39%)
  waiting for transfers between devices  27.9 us (23%)
  matrix products  16.2 us (13%)
  between operations  14.8 us (12%)
  other arithmetic  9.96 us (8%)
  local copies, waits for them, and re-layouts  4.65 us (4%)
    all_gather x2, blocking collectives, local(): whole = lax.all_gather(rounded, 'row', axis=1, tiled=True)  31.3 us
    reduce_scatter x2, waiting for transfers between devices, local(): lax.psum_scatter(jnp.einsum('sr,sli->lri', row_hot, terms, precision=lax....  27.8 us
    unnamed x1, blocking collectives  16.6 us
    dot_general x2, matrix products, local(): jnp.einsum('lsj,sij->sli', picked, tiles, preferred_element_type=jnp.floa...  12.3 us
    reduce_sum x1, other arithmetic, local(): rowsum = jnp.sum(tiles, axis=2, dtype=jnp.float32)  5.11 us
    dot_general x2, matrix products, local(): jnp.einsum('sr,sli->lri', row_hot, terms, precision=lax.Precision.HIGHEST)  3.61 us
    unnamed x11, local copies, waits for them, and re-layouts  2.82 us
  transfers between devices with their start and end apart: 2, of which 2 were waited for; matrix products, arithmetic and copies ran while one was open for 5% of the time, Pallas kernels for 0%

commit v1 on v0

--- a/solution.py
+++ b/solution.py
@@ -2,6 +2,7 @@
 import jax.numpy as jnp
 from jax import lax
 from jax.sharding import PartitionSpec as P
+from jax.lax import axis_index, ppermute, psum
 
 ITERS = 2
 spread_weight = 0.9
@@ -27,7 +28,28 @@
     remaining = ITERS
     for step in range(remaining):
         rounded = current.astype(jnp.bfloat16)
-        whole = lax.all_gather(rounded, "row", axis=1, tiled=True)
+        state_now = psum(1, axis_name="row")
+        r2 = axis_index("row")
+        fresh, z2, main = (state_now, r2, rounded.shape[1])
+        row_list = [no * fresh if b == 1 else no for b, no in enumerate(rounded.shape)]
+        whole = lax.dynamic_update_slice_in_dim(
+            jnp.zeros(row_list, rounded.dtype), rounded, z2 * main, axis=1
+        )
+        current_value = formed = rounded
+        for dev_i in range(1, fresh // 2 + 1):
+            current_value = ppermute(
+                current_value, axis_name="row", perm=[(b, (b + 1) % fresh) for b in range(fresh)]
+            )
+            whole = lax.dynamic_update_slice_in_dim(
+                whole, current_value, (z2 - dev_i) % fresh * main, axis=1
+            )
+            if 2 * dev_i < fresh:
+                formed = ppermute(
+                    formed, axis_name="row", perm=[(b, (b - 1) % fresh) for b in range(fresh)]
+                )
+                whole = lax.dynamic_update_slice_in_dim(
+                    whole, formed, (z2 + dev_i) % fresh * main, axis=1
+                )
         blocks = whole.reshape(labels, -1, tile_size)
         picked = jnp.take(blocks, tile_cols, axis=1)
         terms = jnp.einsum("lsj,sij->sli", picked, tiles, preferred_element_type=jnp.float32)

time: 122 us -> 130 us (1.066)
  blocking collectives: 48 us -> 17 us
  starting transfers between devices: 0.04 us -> 22.9 us
  waiting for transfers between devices: 27.9 us -> 43.4 us
    all_gather x2 -> x0, blocking collectives: 31.3 us -> none  [local(): whole = lax.all_gather(rounded, 'row', axis=1, tiled=True)]
    ppermute x0 -> x14, starting transfers between devices: none -> 22.8 us  [the longest x6 22.2 us: local(): ppermute(formed, axis_name='row', perm=[(b, (b - 1) % fresh) for b in ran...]
    ppermute x0 -> x14, waiting for transfers between devices: none -> 21 us  [the longest x8 20.3 us: local(): ppermute(current_value, axis_name='row', perm=[(b, (b + 1) % fresh) for b...]
    reduce_scatter x2, waiting for transfers between devices: 27.8 us -> 22.4 us  [local(): lax.psum_scatter(jnp.einsum('sr,sli->lri', row_hot, terms, precision=lax....]
    dynamic_update_slice x0 -> x2, other arithmetic: none -> 1.87 us  [local(): lax.dynamic_update_slice_in_dim(jnp.zeros(row_list, rounded.dtype), round...]
    convert_element_type x2 -> x0, other arithmetic: 1.85 us -> none  [local(): rounded = current.astype(jnp.bfloat16)]
  transfers between devices with their start and end apart: 2 -> 16, of which waited for: 2 -> 11; matrix products, arithmetic and copies ran while one was open for 5% -> 6% of each run, Pallas kernels for 0% -> 0%
where the time goes in v1:
time: 130 us; the launch traced here: 129 us
  waiting for transfers between devices  43.4 us (33%)
  starting transfers between devices  22.9 us (18%)
  blocking collectives  17 us (13%)
  matrix products  16.2 us (12%)
  between operations  15 us (12%)
  other arithmetic  9.98 us (8%)
  local copies, waits for them, and re-layouts  4.83 us (4%)
    reduce_scatter x2, waiting for transfers between devices, local(): lax.psum_scatter(jnp.einsum('sr,sli->lri', row_hot, terms, precision=lax....  22.4 us
    ppermute x6, starting transfers between devices, local(): ppermute(formed, axis_name='row', perm=[(b, (b - 1) % fresh) for b in ran...  22.2 us
    ppermute x8, waiting for transfers between devices, local(): ppermute(current_value, axis_name='row', perm=[(b, (b + 1) % fresh) for b...  20.3 us
    unnamed x1, blocking collectives  17 us
    dot_general x2, matrix products, local(): jnp.einsum('lsj,sij->sli', picked, tiles, preferred_element_type=jnp.floa...  12.4 us
    reduce_sum x1, other arithmetic, local(): rowsum = jnp.sum(tiles, axis=2, dtype=jnp.float32)  5.11 us
    dot_general x2, matrix products, local(): jnp.einsum('sr,sli->lri', row_hot, terms, precision=lax.Precision.HIGHEST)  3.6 us
    unnamed x11, local copies, waits for them, and re-layouts  2.81 us
  transfers between devices with their start and end apart: 16, of which 11 were waited for; matrix products, arithmetic and copies ran while one was open for 6% of the time, Pallas kernels for 0%

profile of v1, /device:TPU:0, one launch (start us, length us, event | category | flops | bytes accessed | tf_op | source)
XLA Modules:
  0.0 129.3 jit_solution(5048169297023790315)
XLA Ops:
  6.5 0.0 reduce-scatter.3.cloned.1.call-start
  6.6 0.9 constant_dynamic-update-slice_fusion.15
  7.5 0.5 collective-permute-start
  8.0 4.1 %collective-permute-start.1 = (bf16[16,2048]{1,0:T(8,128)(2,1)S(1)}, bf16[16,2048]{1,0:T(8,128)(2,1)S(1)}, u32[]{:S(2)}, u32[]{:S(2)}) collective-permute-start(bf16[16,2048]{1,0:T(8,128)(2,1)S(1)} %get-tuple-element.9), channel_id=1, source_target_pairs={{0,28},{4,0},{8,4},{12,8},{16,12},{20,16},{24,20},{28,24},{1,29},{... | collective-permute-start | bytes 196616 | tf_op jit(solution)/shard_map/ppermute | solution.py:47
  12.1 0.7 compare_select_fusion
  12.8 0.7 compare_and_fusion
  14.2 0.0 collective-permute-done
  14.2 0.1 collective-permute-start.2
  14.3 0.0 collective-permute-done.1
  14.3 3.5 %collective-permute-start.3 = (bf16[16,2048]{1,0:T(8,128)(2,1)S(1)}, bf16[16,2048]{1,0:T(8,128)(2,1)S(1)}, u32[]{:S(2)}, u32[]{:S(2)}) collective-permute-start(bf16[16,2048]{1,0:T(8,128)(2,1)S(1)} %collective-permute-done.1), channel_id=1, source_target_pairs={{0,28},{4,0},{8,4},{12,8},{16,12},{20,16},{24,20},{28,24},{1,29},{... | collective-permute-start | bytes 196616 | tf_op jit(solution)/shard_map/ppermute | solution.py:47
  17.8 2.0 %collective-permute-done.2 = bf16[16,2048]{1,0:T(8,128)(2,1)S(1)} collective-permute-done((bf16[16,2048]{1,0:T(8,128)(2,1)S(1)}, bf16[16,2048]{1,0:T(8,128)(2,1)S(1)}, u32[]{:S(2)}, u32[]{:S(2)}) %collective-permute-start.2) | collective-permute-done | bytes 65568 | tf_op jit(solution)/shard_map/ppermute | solution.py:40
  19.8 0.0 collective-permute-start.4
  19.9 0.2 collective-permute-done.3
  20.1 3.8 %collective-permute-start.5 = (bf16[16,2048]{1,0:T(8,128)(2,1)S(1)}, bf16[16,2048]{1,0:T(8,128)(2,1)S(1)}, u32[]{:S(2)}, u32[]{:S(2)}) collective-permute-start(bf16[16,2048]{1,0:T(8,128)(2,1)S(1)} %collective-permute-done.3), channel_id=1, source_target_pairs={{0,28},{4,0},{8,4},{12,8},{16,12},{20,16},{24,20},{28,24},{1,29},{... | collective-permute-start | bytes 196616 | tf_op jit(solution)/shard_map/ppermute | solution.py:47
  23.9 1.4 %collective-permute-done.4 = bf16[16,2048]{1,0:T(8,128)(2,1)S(1)} collective-permute-done((bf16[16,2048]{1,0:T(8,128)(2,1)S(1)}, bf16[16,2048]{1,0:T(8,128)(2,1)S(1)}, u32[]{:S(2)}, u32[]{:S(2)}) %collective-permute-start.4) | collective-permute-done | bytes 65568 | tf_op jit(solution)/shard_map/ppermute | solution.py:40
  25.3 0.0 collective-permute-start.6
  25.4 0.5 collective-permute-done.5
  25.8 5.0 %collective-permute-done.6 = bf16[16,2048]{1,0:T(8,128)(2,1)S(1)} collective-permute-done((bf16[16,2048]{1,0:T(8,128)(2,1)S(1)}, bf16[16,2048]{1,0:T(8,128)(2,1)S(1)}, u32[]{:S(2)}, u32[]{:S(2)}) %collective-permute-start.6) | collective-permute-done | bytes 65568 | tf_op jit(solution)/shard_map/ppermute | solution.py:40
  30.8 0.1 copy_bitcast_fusion.3
  30.9 0.8 gather_fusion
  31.8 0.0 copy-start.2
  31.8 6.2 %fusion.6 = f32[224,16,128]{2,1,0:T(8,128)S(1)} fusion(bf16[224,128,128]{2,1,0:T(8,128)(2,1)} %param.8, bf16[224,16,128]{2,1,0:T(8,128)(2,1)S(1)} %gather_fusion, pred[224]{0:T(512)(128)(4,1)S(1)} %compare_and_fusion), kind=kOutput, calls=%fused_computation.10 | convolution fusion | flops 117899264 | bytes 10092768 | tf_op jit(solution)/shard_map/lsj,sij->sli/dot_general | solution.py:55
  38.0 0.0 copy-done.2
  38.0 0.0 copy-start.3
  38.0 1.8 %fusion.2 = f32[16,128,64]{1,2,0:T(8,128)S(1)} fusion(f32[224,16,128]{2,1,0:T(8,128)S(1)} %fusion.6, f32[224]{0:T(256)S(1)} %compare_convert_fusion, s32[224]{0:T(256)S(1)} %copy-done.2), kind=kOutput, calls=%fused_computation.5 | convolution fusion | flops 352350208 | bytes 2361088 | tf_op jit(solution)/shard_map/sr,sli->lri/dot_general | solution.py:57
  39.8 1.1 copy.27
  40.9 0.0 reduce-scatter.3.cloned.1.call-update
  40.9 0.0 reduce-scatter.5.cloned.1.call-start
  41.0 0.0 copy-done.3
  41.0 0.6 dynamic-slice
  42.2 0.0 copy-start
  42.2 5.1 %convert_reduce_fusion = f32[224,128]{1,0:T(8,128)S(1)} fusion(bf16[224,128,128]{2,1,0:T(8,128)(2,1)} %param.8), kind=kLoop, calls=%fused_computation.2 | loop fusion | flops 7311360 | bytes 7454720 | tf_op jit(solution)/shard_map/reduce_sum | solution.py:22
  47.3 0.3 convolution_bitcast_fusion
  47.6 17.0 %all-reduce = f32[8192]{0:T(1024)S(1)} all-reduce(f32[8192]{0:T(1024)S(1)} %convolution_bitcast_fusion), channel_id=3, replica_groups=mesh['row'=8,'col'=4] {'col'}, use_global_device_ids=true, to_apply=%region_2.4.clone | all-reduce | flops 8192 | bytes 65536
  64.6 0.2 reduce-scatter.3.cloned.1.call-done
  64.9 0.0 copy-done
  64.9 0.9 constant_dynamic-update-slice_fusion.7
  65.8 0.1 collective-permute-start.7
  65.9 3.5 %collective-permute-start.8 = (bf16[16,2048]{1,0:T(8,128)(2,1)S(1)}, bf16[16,2048]{1,0:T(8,128)(2,1)S(1)}, u32[]{:S(2)}, u32[]{:S(2)}) collective-permute-start(bf16[16,2048]{1,0:T(8,128)(2,1)S(1)} %get-tuple-element.7), channel_id=1, source_target_pairs={{0,28},{4,0},{8,4},{12,8},{16,12},{20,16},{24,20},{28,24},{1,29},{... | collective-permute-start | bytes 196616 | tf_op jit(solution)/shard_map/ppermute | solution.py:47
  69.4 2.1 %collective-permute-done.7 = bf16[16,2048]{1,0:T(8,128)(2,1)S(1)} collective-permute-done((bf16[16,2048]{1,0:T(8,128)(2,1)S(1)}, bf16[16,2048]{1,0:T(8,128)(2,1)S(1)}, u32[]{:S(2)}, u32[]{:S(2)}) %collective-permute-start.7) | collective-permute-done | bytes 65568 | tf_op jit(solution)/shard_map/ppermute | solution.py:40
  71.5 0.0 collective-permute-start.9
  71.5 0.0 collective-permute-done.8
  71.5 3.6 %collective-permute-start.10 = (bf16[16,2048]{1,0:T(8,128)(2,1)S(1)}, bf16[16,2048]{1,0:T(8,128)(2,1)S(1)}, u32[]{:S(2)}, u32[]{:S(2)}) collective-permute-start(bf16[16,2048]{1,0:T(8,128)(2,1)S(1)} %collective-permute-done.8), channel_id=1, source_target_pairs={{0,28},{4,0},{8,4},{12,8},{16,12},{20,16},{24,20},{28,24},{1,29},{... | collective-permute-start | bytes 196616 | tf_op jit(solution)/shard_map/ppermute | solution.py:47
  75.1 2.5 %collective-permute-done.9 = bf16[16,2048]{1,0:T(8,128)(2,1)S(1)} collective-permute-done((bf16[16,2048]{1,0:T(8,128)(2,1)S(1)}, bf16[16,2048]{1,0:T(8,128)(2,1)S(1)}, u32[]{:S(2)}, u32[]{:S(2)}) %collective-permute-start.9) | collective-permute-done | bytes 65568 | tf_op jit(solution)/shard_map/ppermute | solution.py:40
  77.7 0.0 collective-permute-start.11
  77.7 0.0 collective-permute-done.10
  77.7 3.6 %collective-permute-start.12 = (bf16[16,2048]{1,0:T(8,128)(2,1)S(1)}, bf16[16,2048]{1,0:T(8,128)(2,1)S(1)}, u32[]{:S(2)}, u32[]{:S(2)}) collective-permute-start(bf16[16,2048]{1,0:T(8,128)(2,1)S(1)} %collective-permute-done.10), channel_id=1, source_target_pairs={{0,28},{4,0},{8,4},{12,8},{16,12},{20,16},{24,20},{28,24},{1,29},{... | collective-permute-start | bytes 196616 | tf_op jit(solution)/shard_map/ppermute | solution.py:47
  81.3 1.9 %collective-permute-done.11 = bf16[16,2048]{1,0:T(8,128)(2,1)S(1)} collective-permute-done((bf16[16,2048]{1,0:T(8,128)(2,1)S(1)}, bf16[16,2048]{1,0:T(8,128)(2,1)S(1)}, u32[]{:S(2)}, u32[]{:S(2)}) %collective-permute-start.11) | collective-permute-done | bytes 65568 | tf_op jit(solution)/shard_map/ppermute | solution.py:40
  83.1 0.0 collective-permute-start.13
  83.2 0.0 collective-permute-done.12
  83.2 5.4 %collective-permute-done.13 = bf16[16,2048]{1,0:T(8,128)(2,1)S(1)} collective-permute-done((bf16[16,2048]{1,0:T(8,128)(2,1)S(1)}, bf16[16,2048]{1,0:T(8,128)(2,1)S(1)}, u32[]{:S(2)}, u32[]{:S(2)}) %collective-permute-start.13) | collective-permute-done | bytes 65568 | tf_op jit(solution)/shard_map/ppermute | solution.py:40
  88.6 0.1 copy_bitcast_fusion.2
  88.7 0.8 gather_fusion.1
  89.6 6.2 %fusion.4 = f32[224,16,128]{2,1,0:T(8,128)S(1)} fusion(bf16[224,128,128]{2,1,0:T(8,128)(2,1)} %param.8, bf16[224,16,128]{2,1,0:T(8,128)(2,1)S(1)} %gather_fusion.1, pred[224]{0:T(512)(128)(4,1)S(1)} %compare_and_fusion), kind=kOutput, calls=%fused_computation.8 | convolution fusion | flops 117899264 | bytes 10092768 | tf_op jit(solution)/shard_map/lsj,sij->sli/dot_general | solution.py:55
  95.8 0.0 copy-start.1
  95.8 1.8 %fusion = f32[16,128,64]{1,2,0:T(8,128)S(1)} fusion(f32[224,16,128]{2,1,0:T(8,128)S(1)} %fusion.4, f32[224]{0:T(256)S(1)} %compare_convert_fusion, s32[224]{0:T(256)S(1)} %copy-done.2), kind=kOutput, calls=%fused_computation.3 | convolution fusion | flops 352350208 | bytes 2361088 | tf_op jit(solution)/shard_map/sr,sli->lri/dot_general | solution.py:57
  97.6 1.1 copy.26
  98.7 0.0 reduce-scatter.5.cloned.1.call-update
  98.7 22.2 %reduce-scatter.5.cloned.1.call-done = f32[16,2048]{1,0:T(8,128)} async-done(((f32[16,8192]{1,0:T(8,128)}), f32[16,2048]{1,0:T(8,128)}) %reduce-scatter.5.cloned.1.call-update) | async-done | bytes 131088 | tf_op jit(solution)/shard_map/reduce_scatter | solution.py:56
  120.9 0.0 copy-done.1
  120.9 1.6 %divide_add_fusion = f32[16,2048]{1,0:T(8,128)} fusion(f32[16,2048]{1,0:T(8,128)} %reduce-scatter.5.cloned.1.call-done, f32[16,2048]{1,0:T(8,128)S(1)} %copy-done, f32[2048]{0:T(1024)S(1)} %dynamic-slice_add_fusion, f32[16,2048]{1,0:T(8,128)S(1)} %copy-done.1), kind=kLoop, calls=%fused_computation.22 | loop fusion | flops 294912 | bytes 532480 | tf_op jit(solution)/shard_map/add | solution.py:65
  (19 shorter events, 0.2 us)
Async XLA Ops:
  6.5 58.3 %reduce-scatter.3.cloned.1.call-start = ((), (), s32[]{:S(2)}) async-start(), calls=%async_computation.2 | async-start | bytes 655360 | tf_op jit(solution)/shard_map/reduce_scatter | solution.py:56
  7.5 6.7 %collective-permute-start = (bf16[16,2048]{1,0:T(8,128)(2,1)S(1)}, bf16[16,2048]{1,0:T(8,128)(2,1)S(1)}, u32[]{:S(2)}, u32[]{:S(2)}) collective-permute-start(bf16[16,2048]{1,0:T(8,128)(2,1)S(1)} %get-tuple-element.9), channel_id=1, source_target_pairs={{0,4},{4,8},{8,12},{12,16},{16,20},{20,24},{24,28},{28,0},{1,5},{5... | collective-permute-start | bytes 196616 | tf_op jit(solution)/shard_map/ppermute | solution.py:40
  8.0 6.3 %collective-permute-start.1 = (bf16[16,2048]{1,0:T(8,128)(2,1)S(1)}, bf16[16,2048]{1,0:T(8,128)(2,1)S(1)}, u32[]{:S(2)}, u32[]{:S(2)}) collective-permute-start(bf16[16,2048]{1,0:T(8,128)(2,1)S(1)} %get-tuple-element.9), channel_id=1, source_target_pairs={{0,28},{4,0},{8,4},{12,8},{16,12},{20,16},{24,20},{28,24},{1,29},{... | collective-permute-start | bytes 196616 | tf_op jit(solution)/shard_map/ppermute | solution.py:47
  14.2 5.6 %collective-permute-start.2 = (bf16[16,2048]{1,0:T(8,128)(2,1)S(1)}, bf16[16,2048]{1,0:T(8,128)(2,1)S(1)}, u32[]{:S(2)}, u32[]{:S(2)}) collective-permute-start(bf16[16,2048]{1,0:T(8,128)(2,1)S(1)} %collective-permute-done), channel_id=1, source_target_pairs={{0,4},{4,8},{8,12},{12,16},{16,20},{20,24},{24,28},{28,0},{1,5},{5... | collective-permute-start | bytes 196616 | tf_op jit(solution)/shard_map/ppermute | solution.py:40
  14.3 5.8 %collective-permute-start.3 = (bf16[16,2048]{1,0:T(8,128)(2,1)S(1)}, bf16[16,2048]{1,0:T(8,128)(2,1)S(1)}, u32[]{:S(2)}, u32[]{:S(2)}) collective-permute-start(bf16[16,2048]{1,0:T(8,128)(2,1)S(1)} %collective-permute-done.1), channel_id=1, source_target_pairs={{0,28},{4,0},{8,4},{12,8},{16,12},{20,16},{24,20},{28,24},{1,29},{... | collective-permute-start | bytes 196616 | tf_op jit(solution)/shard_map/ppermute | solution.py:47
  19.8 5.5 %collective-permute-start.4 = (bf16[16,2048]{1,0:T(8,128)(2,1)S(1)}, bf16[16,2048]{1,0:T(8,128)(2,1)S(1)}, u32[]{:S(2)}, u32[]{:S(2)}) collective-permute-start(bf16[16,2048]{1,0:T(8,128)(2,1)S(1)} %collective-permute-done.2), channel_id=1, source_target_pairs={{0,4},{4,8},{8,12},{12,16},{16,20},{20,24},{24,28},{28,0},{1,5},{5... | collective-permute-start | bytes 196616 | tf_op jit(solution)/shard_map/ppermute | solution.py:40
  20.1 5.7 %collective-permute-start.5 = (bf16[16,2048]{1,0:T(8,128)(2,1)S(1)}, bf16[16,2048]{1,0:T(8,128)(2,1)S(1)}, u32[]{:S(2)}, u32[]{:S(2)}) collective-permute-start(bf16[16,2048]{1,0:T(8,128)(2,1)S(1)} %collective-permute-done.3), channel_id=1, source_target_pairs={{0,28},{4,0},{8,4},{12,8},{16,12},{20,16},{24,20},{28,24},{1,29},{... | collective-permute-start | bytes 196616 | tf_op jit(solution)/shard_map/ppermute | solution.py:47
  25.3 5.5 %collective-permute-start.6 = (bf16[16,2048]{1,0:T(8,128)(2,1)S(1)}, bf16[16,2048]{1,0:T(8,128)(2,1)S(1)}, u32[]{:S(2)}, u32[]{:S(2)}) collective-permute-start(bf16[16,2048]{1,0:T(8,128)(2,1)S(1)} %collective-permute-done.4), channel_id=1, source_target_pairs={{0,4},{4,8},{8,12},{12,16},{16,20},{20,24},{24,28},{28,0},{1,5},{5... | collective-permute-start | bytes 196616 | tf_op jit(solution)/shard_map/ppermute | solution.py:40
  31.8 6.2 %copy-start.2 = (s32[224]{0:T(256)S(1)}, s32[224]{0:T(256)}, u32[]{:S(2)}) copy-start(s32[224]{0:T(256)} %param.9) | copy-start | bytes 2692
  38.0 3.0 %copy-start.3 = (u32[32]{0:T(128)S(1)}, u32[32]{0:T(128)}, u32[]{:S(2)}) copy-start(u32[32]{0:T(128)} %constant.101) | copy-start | bytes 388
  40.9 80.0 %reduce-scatter.5.cloned.1.call-start = ((), (), s32[]{:S(2)}) async-start(), calls=%async_computation.3 | async-start | bytes 655360 | tf_op jit(solution)/shard_map/reduce_scatter | solution.py:56
  42.2 22.7 %copy-start = (f32[16,2048]{1,0:T(8,128)S(1)}, f32[16,2048]{1,0:T(8,128)}, u32[]{:S(2)}) copy-start(f32[16,2048]{1,0:T(8,128)} %param.7) | copy-start | bytes 393220
  65.8 5.6 %collective-permute-start.7 = (bf16[16,2048]{1,0:T(8,128)(2,1)S(1)}, bf16[16,2048]{1,0:T(8,128)(2,1)S(1)}, u32[]{:S(2)}, u32[]{:S(2)}) collective-permute-start(bf16[16,2048]{1,0:T(8,128)(2,1)S(1)} %get-tuple-element.7), channel_id=1, source_target_pairs={{0,4},{4,8},{8,12},{12,16},{16,20},{20,24},{24,28},{28,0},{1,5},{5... | collective-permute-start | bytes 196616 | tf_op jit(solution)/shard_map/ppermute | solution.py:40
  65.9 5.6 %collective-permute-start.8 = (bf16[16,2048]{1,0:T(8,128)(2,1)S(1)}, bf16[16,2048]{1,0:T(8,128)(2,1)S(1)}, u32[]{:S(2)}, u32[]{:S(2)}) collective-permute-start(bf16[16,2048]{1,0:T(8,128)(2,1)S(1)} %get-tuple-element.7), channel_id=1, source_target_pairs={{0,28},{4,0},{8,4},{12,8},{16,12},{20,16},{24,20},{28,24},{1,29},{... | collective-permute-start | bytes 196616 | tf_op jit(solution)/shard_map/ppermute | solution.py:47
  71.5 6.2 %collective-permute-start.9 = (bf16[16,2048]{1,0:T(8,128)(2,1)S(1)}, bf16[16,2048]{1,0:T(8,128)(2,1)S(1)}, u32[]{:S(2)}, u32[]{:S(2)}) collective-permute-start(bf16[16,2048]{1,0:T(8,128)(2,1)S(1)} %collective-permute-done.7), channel_id=1, source_target_pairs={{0,4},{4,8},{8,12},{12,16},{16,20},{20,24},{24,28},{28,0},{1,5},{5... | collective-permute-start | bytes 196616 | tf_op jit(solution)/shard_map/ppermute | solution.py:40
  71.5 6.2 %collective-permute-start.10 = (bf16[16,2048]{1,0:T(8,128)(2,1)S(1)}, bf16[16,2048]{1,0:T(8,128)(2,1)S(1)}, u32[]{:S(2)}, u32[]{:S(2)}) collective-permute-start(bf16[16,2048]{1,0:T(8,128)(2,1)S(1)} %collective-permute-done.8), channel_id=1, source_target_pairs={{0,28},{4,0},{8,4},{12,8},{16,12},{20,16},{24,20},{28,24},{1,29},{... | collective-permute-start | bytes 196616 | tf_op jit(solution)/shard_map/ppermute | solution.py:47
  77.7 5.5 %collective-permute-start.11 = (bf16[16,2048]{1,0:T(8,128)(2,1)S(1)}, bf16[16,2048]{1,0:T(8,128)(2,1)S(1)}, u32[]{:S(2)}, u32[]{:S(2)}) collective-permute-start(bf16[16,2048]{1,0:T(8,128)(2,1)S(1)} %collective-permute-done.9), channel_id=1, source_target_pairs={{0,4},{4,8},{8,12},{12,16},{16,20},{20,24},{24,28},{28,0},{1,5},{5... | collective-permute-start | bytes 196616 | tf_op jit(solution)/shard_map/ppermute | solution.py:40
  77.7 5.5 %collective-permute-start.12 = (bf16[16,2048]{1,0:T(8,128)(2,1)S(1)}, bf16[16,2048]{1,0:T(8,128)(2,1)S(1)}, u32[]{:S(2)}, u32[]{:S(2)}) collective-permute-start(bf16[16,2048]{1,0:T(8,128)(2,1)S(1)} %collective-permute-done.10), channel_id=1, source_target_pairs={{0,28},{4,0},{8,4},{12,8},{16,12},{20,16},{24,20},{28,24},{1,29},{... | collective-permute-start | bytes 196616 | tf_op jit(solution)/shard_map/ppermute | solution.py:47
  83.1 5.5 %collective-permute-start.13 = (bf16[16,2048]{1,0:T(8,128)(2,1)S(1)}, bf16[16,2048]{1,0:T(8,128)(2,1)S(1)}, u32[]{:S(2)}, u32[]{:S(2)}) collective-permute-start(bf16[16,2048]{1,0:T(8,128)(2,1)S(1)} %collective-permute-done.11), channel_id=1, source_target_pairs={{0,4},{4,8},{8,12},{12,16},{16,20},{20,24},{24,28},{28,0},{1,5},{5... | collective-permute-start | bytes 196616 | tf_op jit(solution)/shard_map/ppermute | solution.py:40
  95.8 25.1 %copy-start.1 = (f32[16,2048]{1,0:T(8,128)S(1)}, f32[16,2048]{1,0:T(8,128)}, u32[]{:S(2)}) copy-start(f32[16,2048]{1,0:T(8,128)} %reduce-scatter.3.cloned.1.call-done) | copy-start | bytes 393220
Sparse Core Ops, SparseCore 0:
  41.0 23.7 reduce-scatter.2
  98.8 22.0 reduce-scatter.4
